TPU v7x, 32 devices: a whole 2x2x4 slice. The times are simulated.
32 devices in a mesh: cls: 16 (over z, y, x), dp: 2 (over core).
Axes of the slice: x: 2, y: 2, z: 4, core: 2. Of those that a mesh axis runs over, the one named last changes fastest.
Arguments:
- images: bfloat16 [512, 4096], P(('cls', 'dp')), may hold values from -6 to 6
- references: bfloat16 [16, 72, 4096], P('cls'), may hold values from -1 to 1
- candidates: int32 [512, 8], P(('cls', 'dp')), may hold values from 0 to 15, all different within a row; in each aligned block of 16 rows (0 to 15, 16 to 31, ...) at most 12 rows name the same one
- inv_noise: bfloat16 [512], P(('cls', 'dp')), may hold values from 0.5 to 150
Outputs:
- class_sums: float32 [16, 72, 4096], P('cls', 'dp')
- class_weights: float32 [16, 72], P('cls', 'dp')
Inputs may be any that keep to these rules, and one draw needn't show every extreme that they name: `candidates`: the classes of one row differ. In each aligned block of 16 rows (the rows of one device) no class is named by more than 12 rows, a bound that some block reaches.
All inputs are finite; a program needn't handle non-finite values.
Results may differ from a plain program's by a relative error of at most 0.006.
Values may be sent and summed in bfloat16 or wider, within the bound.
A program may use at most 64 MiB of HBM per device.

v0:
```python
import functools
import math

import jax
import jax.numpy as jnp
from jax import lax
from jax.experimental import pallas as pl
from jax.experimental.pallas import tpu as pltpu
from jax.sharding import PartitionSpec as P

MESH = pl.DeviceIdType.MESH
LANES = 128
LOW = -1e30

OFFSETS = ((0, 0), (1, 0), (-1, 0), (0, 1), (0, -1), (1, 1), (1, -1), (-1, 1), (-1, -1))


def roll_flat(rows, shift_row, shift_col, side_len):
    result = jnp.roll(rows, shift_row * side_len, axis=1)
    if shift_col != 0:
        column = jnp.arange(side_len * side_len, dtype=jnp.int32) % side_len
        edge = 0 if shift_col > 0 else side_len - 1
        wrapped = jnp.roll(result, shift_col - shift_col * side_len, axis=1)
        plain = jnp.roll(result, shift_col, axis=1)
        result = jnp.where((column == edge)[None, :], wrapped, plain)
    return result


def shift_stack(rotated, side_len):
    return jnp.concatenate(
        [roll_flat(rotated, shift_row, shift_col, side_len) for shift_row, shift_col in OFFSETS],
        axis=0,
    )


def unshift_sum(summed_back, rot_count, side_len):
    square = summed_back.reshape(len(OFFSETS), rot_count, side_len * side_len)
    result = jnp.zeros((rot_count, side_len * side_len), jnp.float32)
    for position, offset in enumerate(OFFSETS):
        result = result + roll_flat(square[position], -offset[0], -offset[1], side_len)
    return result


def on_device(images, references, candidates, inv_noise):
    rows_dev, top_count = candidates.shape
    cls_dev, rot_count, pixels = references.shape
    side_len = math.isqrt(pixels)
    shift_count = len(OFFSETS)
    orient_count = rot_count * shift_count
    n_cls = lax.axis_size("cls")
    classes = cls_dev * n_cls
    slot_depth = max(2, (3 * rows_dev * top_count + 2 * classes - 1) // (2 * classes))
    owner_slots = cls_dev * slot_depth
    slots_all = n_cls * owner_slots
    member = jnp.sum(
        (candidates[:, :, None] == jnp.arange(classes, dtype=jnp.int32)[None, None, :]).astype(
            jnp.int32
        ),
        axis=1,
    )
    before = jnp.cumsum(member, axis=0) - member
    slot_rank = jnp.take_along_axis(before, candidates, axis=1)
    slot_index = candidates // cls_dev * owner_slots + candidates % cls_dev * slot_depth + slot_rank
    flat_slot = slot_index.reshape(-1)
    source = (
        jnp.full((slots_all,), rows_dev, jnp.int32)
        .at[flat_slot]
        .set(jnp.repeat(jnp.arange(rows_dev, dtype=jnp.int32), top_count))
    )
    images_pad = jnp.concatenate([images, jnp.zeros((1, pixels), jnp.bfloat16)], axis=0)
    noise_pad = jnp.concatenate([inv_noise, jnp.zeros((1,), jnp.bfloat16)], axis=0)
    send_img = images_pad[source].reshape(n_cls, owner_slots * pixels)
    send_noise = noise_pad[source].reshape(n_cls, owner_slots)
    recv_img, recv_noise = (
        lax.all_to_all(send_img, "cls", split_axis=0, concat_axis=0, tiled=True),
        lax.all_to_all(send_noise, "cls", split_axis=0, concat_axis=0, tiled=True),
    )
    live_list = []
    class_pos = 0
    rows_img = recv_img.reshape(n_cls * slot_depth, pixels)
    rows_noise = recv_noise.reshape(-1).astype(jnp.float32)
    shifted = shift_stack(references[class_pos], side_len)
    ref_norms = jnp.sum(jnp.square(references[class_pos].astype(jnp.float32)), axis=1)
    products = lax.dot_general(
        rows_img, shifted, (((1,), (1,)), ((), ())), preferred_element_type=jnp.float32
    )
    class_scores = rows_noise[:, None] * (
        products - 0.5 * jnp.tile(ref_norms, shift_count)[None, :]
    )
    rows_list = [rows_img]
    live_list.append(rows_noise > 0)
    score_list = [class_scores]
    send_scores = jnp.concatenate(
        [part_scores.reshape(n_cls, slot_depth * orient_count) for part_scores in score_list],
        axis=1,
    )
    home_scores = lax.all_to_all(send_scores, "cls", split_axis=0, concat_axis=0, tiled=True)
    own_scores = home_scores.reshape(slots_all, orient_count)[slot_index]
    row_peak = jnp.max(own_scores, axis=(1, 2))
    norm_total = jnp.sum(jnp.exp(own_scores - row_peak[:, None, None]), axis=(1, 2))
    home_weights = (
        jnp.exp(own_scores - row_peak[:, None, None]) / norm_total[:, None, None]
    ).astype(jnp.bfloat16)
    slot_weights = (
        jnp.zeros((slots_all, orient_count), jnp.bfloat16)
        .at[flat_slot]
        .set(home_weights.reshape(-1, orient_count))
    )
    weights = lax.all_to_all(
        slot_weights.reshape(n_cls, owner_slots * orient_count),
        "cls",
        split_axis=0,
        concat_axis=0,
        tiled=True,
    )
    weight_rows = [weights.reshape(n_cls * slot_depth, orient_count)]
    class_pos = 0
    row_weights = weight_rows[class_pos]
    summed_back = lax.dot_general(
        row_weights,
        rows_list[class_pos],
        (((0,), (0,)), ((), ())),
        preferred_element_type=jnp.float32,
    )
    sums_list = [unshift_sum(summed_back, rot_count, side_len)]
    weight_list = [
        jnp.sum(row_weights.astype(jnp.float32), axis=0).reshape(shift_count, rot_count).sum(axis=0)
    ]
    local_sums = jnp.stack(sums_list, axis=0)
    local_weights = jnp.stack(weight_list, axis=0)
    class_sums, class_weights = (
        lax.psum_scatter(local_sums, "dp", scatter_dimension=1, tiled=True),
        lax.psum_scatter(local_weights, "dp", scatter_dimension=1, tiled=True),
    )
    return (class_sums, class_weights)


PLANES = 4


def dense_kernel(
    rows_dev, pixels, half, pad, side, n_cls,
    own_ref, ref_ref, sums_ref, tot_ref,
    held, shifted, norms, acc, expo, back, mine, stats,
    own_sem, col_send, col_recv, x_send, y_send, a_recv, b_recv, part_send, part_recv,
    st_send, st_recv,
):
    cls = lax.axis_index("cls")
    d = lax.axis_index("dp")
    z, y, x = cls // 4, (cls // 2) % 2, cls % 2
    other = 1 - d
    me = cls * 2 + d
    n_dev = n_cls * 2
    width = held.shape[2]
    cut = (width // 2 + LANES - 1) // LANES * LANES
    part_a, part_b = pl.ds(0, cut), pl.ds(cut, width - cut)

    def block(bz, by, bx):
        return bz * 4 + by * 2 + bx

    barrier = pltpu.get_barrier_semaphore()

    def greet(j, carry):
        t = (me + j) % n_dev
        pl.semaphore_signal(barrier, inc=1, device_id={"cls": t // 2, "dp": t % 2}, device_id_type=MESH)
        return carry

    lax.fori_loop(1, n_dev, greet, 0)
    pl.semaphore_wait(barrier, n_dev - 1)

    t = z // 2
    order = [z, z + 1 - 2 * (z % 2), 2 - t, 3 - 3 * t]
    x_dev = {"cls": block(z, y, 1 - x), "dp": d}
    y_dev = {"cls": block(z, 1 - y, x), "dp": d}
    up_dev = {"cls": jnp.minimum(cls + 4, n_cls - 1) * 0 + (cls + 4) % n_cls, "dp": d}
    down_dev = {"cls": (cls + n_cls - 4) % n_cls, "dp": d}
    core_dev = {"cls": cls, "dp": other}

    def slot(b):
        return d * n_cls + b

    def remote(src, dst, send, recv, dev):
        return pltpu.make_async_remote_copy(
            src_ref=src, dst_ref=dst, send_sem=send, recv_sem=recv, device_id=dev, device_id_type=MESH
        )

    def full(k, which, b, dev):
        src = own_ref if k == 0 else held.at[slot(b)]
        return remote(src, held.at[slot(b)], col_send.at[k, which], col_recv.at[b], dev)

    def to_core(index, b, src=None):
        src = held.at[slot(b)] if src is None else src
        return remote(src, held.at[slot(b)], part_send.at[index], part_recv.at[b], core_dev)

    def piece(b, cols, send, recv, dev):
        ref = held.at[slot(b), :, cols]
        return remote(ref, ref, send, recv.at[b], dev)

    started = []

    def go(copy, cond=None):
        started.append((copy, cond))
        if cond is None:
            copy.start()
        else:
            pl.when(cond)(lambda: copy.start())

    def column_sends(k):
        b = block(order[k], y, x)
        zk = order[k]
        if k == 0:
            up, down = z < PLANES - 1, z > 0
        else:
            up = jnp.logical_and(zk < z, z < PLANES - 1)
            down = jnp.logical_and(zk > z, z > 0)
        go(full(k, 2, b, up_dev), up)
        go(full(k, 3, b, down_dev), down)
        go(full(k, 0, b, x_dev))
        go(full(k, 1, b, y_dev))
        go(to_core(k, b, own_ref if k == 0 else None))

    count = len(OFFSETS)

    def pick_rows():
        row = lax.broadcasted_iota(jnp.int32, (pad, 2 * half), 0)
        col = lax.broadcasted_iota(jnp.int32, (pad, 2 * half), 1)
        pick = jnp.logical_and(col == row + d * half, row < half).astype(jnp.float32).astype(jnp.bfloat16)
        width_c = pixels // 8
        for c in range(8):
            cols = pl.ds(c * width_c, width_c)
            back[0:pad, cols] = jnp.dot(pick, ref_ref[0, :, cols], preferred_element_type=jnp.float32)
        norms[...] = jnp.broadcast_to(
            jnp.sum(jnp.square(back[0:pad, :]), axis=1, keepdims=True), norms.shape
        )

    lane = lax.broadcasted_iota(jnp.int32, (8, pixels), 1) % side

    def rolled(v, dy, dx):
        amount = (dy * side) % pixels
        if dx == 0:
            return v if amount == 0 else pltpu.roll(v, amount, 1)
        plain = pltpu.roll(v, (dy * side + dx) % pixels, 1)
        wrapped = pltpu.roll(v, (dy * side + dx - dx * side) % pixels, 1)
        return jnp.where(lane == (0 if dx > 0 else side - 1), wrapped, plain)

    def build(positions):
        for pair in positions:
            group = [p for p in (2 * pair, 2 * pair + 1) if p < count]
            tiles = []
            for p in group:
                for i in range(pad // 8):
                    tiles.append((p, i))
            if len(tiles) % 2:
                tiles.append(None)
            for q in range(0, len(tiles), 2):
                parts = []
                for item in tiles[q:q + 2]:
                    if item is None:
                        parts.append(jnp.zeros((8, pixels), jnp.float32))
                    else:
                        p, i = item
                        parts.append(rolled(back[8 * i:8 * i + 8, :], *OFFSETS[p]))
                base = 2 * pair * pad + 8 * q
                shifted[base:base + 16, :] = jnp.concatenate(parts, axis=0).astype(jnp.bfloat16)

    local = pltpu.make_async_copy(own_ref, held.at[slot(cls)], own_sem)
    local.start()
    column_sends(0)
    pick_rows()
    build([0])
    for k in range(PLANES):
        xb = block(order[k], y, 1 - x)
        full(k, 0, xb, x_dev).wait_recv() if k else remote(held.at[slot(xb)], held.at[slot(xb)], col_send.at[0, 0], col_recv.at[xb], x_dev).wait_recv()
        go(piece(xb, part_b, x_send.at[k], b_recv, y_dev))
        go(to_core(PLANES + k, xb))
        yb = block(order[k], 1 - y, x)
        remote(held.at[slot(yb)], held.at[slot(yb)], col_send.at[0, 1], col_recv.at[yb], y_dev).wait_recv()
        go(piece(yb, part_a, y_send.at[k], a_recv, x_dev))
        go(to_core(2 * PLANES + k, yb))
        if k + 1 < PLANES:
            zb = block(order[k + 1], y, x)
            remote(held.at[slot(zb)], held.at[slot(zb)], col_send.at[0, 2], col_recv.at[zb], up_dev).wait_recv()
            column_sends(k + 1)
        build([k + 1])
    for k in range(PLANES):
        b = block(order[k], 1 - y, 1 - x)
        piece(b, part_a, y_send.at[k], a_recv, x_dev).wait_recv()
        piece(b, part_b, x_send.at[k], b_recv, y_dev).wait_recv()
        go(to_core(3 * PLANES + k, b))
    local.wait()

    def core_arrival(b, carry):
        s = other * n_cls + b
        remote(held.at[s], held.at[s], part_send.at[0], part_recv.at[b], core_dev).wait_recv()
        return carry

    lax.fori_loop(0, n_cls, core_arrival, 0)
    for copy, cond in started:
        if cond is None:
            copy.wait_send()
        else:
            pl.when(cond)(lambda copy=copy: copy.wait_send())

    n_all = n_dev * rows_dev
    height = shifted.shape[0]
    meta = held[:, :, pixels:pixels + LANES].reshape(n_all, LANES)
    pick = (lax.broadcasted_iota(jnp.int32, (8, LANES), 1) == cls).astype(jnp.float32).astype(jnp.bfloat16)
    noise = lax.dot_general(pick, meta, (((1,), (1,)), ((), ())), preferred_element_type=jnp.float32)[0:1, :]
    depth = pixels // 8

    acc[...] = jnp.zeros_like(acc)

    def chunk(c, carry):
        cols = pl.ds(pl.multiple_of(c * depth, depth), depth)
        right = held[:, :, cols].reshape(n_all, depth)
        acc[...] += lax.dot_general(
            shifted[:, cols], right, (((1,), (1,)), ((), ())), preferred_element_type=jnp.float32
        )
        return carry

    lax.fori_loop(0, 8, chunk, 0)
    rows = count * pad
    prod = acc[0:rows, :].reshape(count, pad, n_all)
    offset = 0.5 * norms[:, 0:1]
    valid = jnp.logical_and(
        noise[None] > 0,
        lax.broadcasted_iota(jnp.int32, (1, pad, n_all), 1) < half,
    )
    score = jnp.where(valid, noise[None] * (prod - offset[None]), LOW)
    peak = jnp.max(jnp.max(score, axis=0), axis=0, keepdims=True)
    grown = jnp.where(valid, jnp.exp(score - peak[None]), 0.0)
    total = jnp.sum(jnp.sum(grown, axis=0), axis=0, keepdims=True)
    mine[0:1, :] = peak
    mine[1:2, :] = total
    expo[...] = grown

    def stat(j):
        t = (me + j) % n_dev
        return remote(mine, stats.at[me], st_send.at[j], st_recv.at[me], {"cls": t // 2, "dp": t % 2})

    def send_stat(j, carry):
        stat(j).start()
        return carry

    stats[me] = mine[...]
    lax.fori_loop(1, n_dev, send_stat, 0)

    def wait_stat(j, carry):
        t = (me + j) % n_dev
        remote(mine, stats.at[t], st_send.at[j], st_recv.at[t], {"cls": t // 2, "dp": t % 2}).wait_recv()
        return carry

    lax.fori_loop(1, n_dev, wait_stat, 0)

    every = stats[...]
    peaks, totals = every[:, 0:1, :], every[:, 1:2, :]
    top = jnp.max(peaks, axis=0)
    norm = jnp.sum(totals * jnp.exp(peaks - top[None]), axis=0)
    factor = jnp.exp(mine[0:1, :] - top) / norm
    weight = (expo[...] * factor[None]).reshape(rows, n_all)
    if height > rows:
        weight = jnp.concatenate([weight, jnp.zeros((height - rows, n_all), jnp.float32)], axis=0)
    weight = weight.astype(jnp.bfloat16)
    flat = jnp.sum(weight[0:rows].astype(jnp.float32).reshape(count, pad, n_all), axis=0)
    column = jnp.sum(flat, axis=1, keepdims=True)
    eye = lax.broadcasted_iota(jnp.int32, (pad, LANES), 0) == lax.broadcasted_iota(jnp.int32, (pad, LANES), 1)
    tot_ref[...] = jnp.sum(jnp.where(eye, column, 0.0), axis=0, keepdims=True)[:, 0:half]
    shifted[:, 0:n_all] = weight

    def project(c, carry):
        cols = pl.ds(pl.multiple_of(c * depth, depth), depth)
        right = held[:, :, cols].reshape(n_all, depth)
        back[:, cols] = jnp.dot(shifted[:, 0:n_all], right, preferred_element_type=jnp.float32)
        return carry

    lax.fori_loop(0, 8, project, 0)

    place = {offset: i for i, offset in enumerate(OFFSETS)}

    def tile(i):
        lines = []
        for dx in (0, 1, -1):
            line = None
            for dy in (0, 1, -1):
                base = place[(dy, dx)] * pad + 8 * i
                term = rolled(back[base:base + 8, :], -dy, 0)
                line = term if line is None else line + term
            lines.append(line)
        return lines[0] + rolled(lines[1], 0, -1) + rolled(lines[2], 0, 1)

    for i in range(pad // 8):
        keep = min(8, half - 8 * i)
        sums_ref[0, 8 * i:8 * i + keep, :] = tile(i)[0:keep]

    def end_stat(j, carry):
        stat(j).wait_send()
        return carry

    lax.fori_loop(1, n_dev, end_stat, 0)


def dense_on_device(images, references, candidates, inv_noise):
    rows_dev, pixels = images.shape
    n_cls, n_dp = lax.axis_size("cls"), lax.axis_size("dp")
    rot_count = references.shape[1]
    half = rot_count // n_dp
    pad = (half + 7) // 8 * 8
    side = math.isqrt(pixels)
    height = (len(OFFSETS) * pad + 15) // 16 * 16
    n_all = rows_dev * n_cls * n_dp
    named = (candidates[:, :, None] == jnp.arange(LANES, dtype=jnp.int32)[None, None, :]).any(axis=1)
    meta = jnp.where(named, inv_noise[:, None], jnp.zeros((), jnp.bfloat16))
    own = jnp.concatenate([images, meta], axis=1)
    width = pixels + LANES
    dma = pltpu.SemaphoreType.DMA
    vmem = pl.BlockSpec(memory_space=pltpu.VMEM)
    return pl.pallas_call(
        functools.partial(dense_kernel, rows_dev, pixels, half, pad, side, n_cls),
        out_shape=(
            jax.ShapeDtypeStruct((1, half, pixels), jnp.float32),
            jax.ShapeDtypeStruct((1, half), jnp.float32),
        ),
        in_specs=[vmem, vmem],
        out_specs=(vmem, vmem),
        scratch_shapes=[
            pltpu.VMEM((n_cls * n_dp, rows_dev, width), jnp.bfloat16),
            pltpu.VMEM((height, pixels), jnp.bfloat16),
            pltpu.VMEM((pad, LANES), jnp.float32),
            pltpu.VMEM((height, n_all), jnp.float32),
            pltpu.VMEM((len(OFFSETS), pad, n_all), jnp.float32),
            pltpu.VMEM((height, pixels), jnp.float32),
            pltpu.VMEM((2, n_all), jnp.float32),
            pltpu.VMEM((n_cls * n_dp, 2, n_all), jnp.float32),
            dma,
            dma((PLANES, 4)),
            dma((n_cls,)),
            dma((PLANES,)),
            dma((PLANES,)),
            dma((n_cls,)),
            dma((n_cls,)),
            dma((4 * PLANES,)),
            dma((n_cls,)),
            dma((n_cls * n_dp,)),
            dma((n_cls * n_dp,)),
        ],
        compiler_params=pltpu.CompilerParams(
            collective_id=0, has_side_effects=True, vmem_limit_bytes=56 << 20
        ),
    )(own, references)


def solution(mesh):
    placed = (
        P(("cls", "dp"), None),
        P("cls", None, None),
        P(("cls", "dp"), None),
        P(("cls", "dp")),
    )
    n_cls, n_dp = mesh.shape["cls"], mesh.shape["dp"]
    dense = n_cls == PLANES * 4 and n_dp == 2
    return jax.shard_map(
        dense_on_device if dense else on_device,
        mesh=mesh,
        in_specs=placed,
        out_specs=(P("cls", "dp", None), P("cls", "dp")),
        check_vma=False,
    )
```

profile of v0, /device:TPU:0, one launch (start us, length us, event | category | flops | bytes accessed | tf_op | source)
XLA Modules:
  0.0 58.9 jit_solution(11871079692301875505)
XLA Ops:
  0.6 0.8 %copy.8 = s32[16,8]{1,0:T(8,128)S(1)} copy(s32[16,8]{0,1:T(8,128)} %param.6) | data formatting | bytes 1024 | tf_op args[2]
  1.4 0.0 copy-start
  1.4 0.1 fusion
  1.5 0.6 copy-done
  2.0 0.1 broadcast_select_fusion
  2.1 1.6 %pad_maximum_fusion.own_ref = bf16[16,4224]{1,0:T(8,128)(2,1)} fusion(bf16[16,128]{1,0:T(8,128)(2,1)S(1)} %broadcast_select_fusion, bf16[16,4096]{1,0:T(8,128)(2,1)} %param.4), kind=kLoop, calls=%fused_computation | loop fusion | flops 270336 | bytes 270336 | tf_op jit(solution)/shard_map/concatenate | solution.py:413
  3.7 52.2 %shard_map.59 = (f32[1,36,4096]{2,1,0:T(8,128)}, f32[1,36]{1,0:T(1,128)}) custom-call(bf16[16,4224]{1,0:T(8,128)(2,1)} %pad_maximum_fusion.own_ref, bf16[1,72,4096]{2,1,0:T(8,128)(2,1)} %ref_ref.1), custom_call_target="tpu_custom_call" | custom-call | tf_op jit(solution)/shard_map/pallas_call | solution.py:417
  55.9 0.0 copy-start.1
  55.9 2.5 %copy.9 = f32[1,36,4096]{2,0,1:T(1,128)} copy(f32[1,36,4096]{2,1,0:T(8,128)} %get-tuple-element.4) | data formatting | bytes 1179648 | tf_op jit(solution)/shard_map/pallas_call | solution.py:417
  58.4 0.0 copy-done.1
  58.4 0.5 copy.11
Async XLA Ops:
  1.4 0.7 %copy-start = (bf16[16]{0:T(256)(128)(2,1)S(1)}, bf16[16]{0:T(256)(128)(2,1)}, u32[]{:S(2)}) copy-start(bf16[16]{0:T(256)(128)(2,1)} %param.7) | copy-start | bytes 100
  55.9 2.5 %copy-start.1 = (f32[1,36]{1,0:T(1,128)S(1)}, f32[1,36]{1,0:T(1,128)}, u32[]{:S(2)}) copy-start(f32[1,36]{1,0:T(1,128)} %get-tuple-element.9) | copy-start | bytes 436
where the time goes:
time: 59.1 us; the launch traced here: 58.9 us
  Pallas kernels  52.2 us (88%)
  local copies, waits for them, and re-layouts  4.33 us (7%)
  other arithmetic  1.74 us (3%)
  between operations  0.65 us (1%)
    pallas_call x1, Pallas kernels, dense_on_device(): pl.pallas_call(functools.partial(dense_kernel, rows_dev, pixels, half, pa...  52.2 us
    pallas_call x1, local copies, waits for them, and re-layouts, dense_on_device(): pl.pallas_call(functools.partial(dense_kernel, rows_dev, pixels, half, pa...  2.51 us
    unnamed x6, local copies, waits for them, and re-layouts  1.83 us
    concatenate x1, other arithmetic, dense_on_device(): own = jnp.concatenate([images, meta], axis=1)  1.57 us

commit v1 on v0

--- a/solution.py
+++ b/solution.py
@@ -160,21 +160,24 @@
 
     barrier = pltpu.get_barrier_semaphore()
 
-    def greet(j, carry):
-        t = (me + j) % n_dev
-        pl.semaphore_signal(barrier, inc=1, device_id={"cls": t // 2, "dp": t % 2}, device_id_type=MESH)
-        return carry
-
-    lax.fori_loop(1, n_dev, greet, 0)
-    pl.semaphore_wait(barrier, n_dev - 1)
 
     t = z // 2
     order = [z, z + 1 - 2 * (z % 2), 2 - t, 3 - 3 * t]
     x_dev = {"cls": block(z, y, 1 - x), "dp": d}
     y_dev = {"cls": block(z, 1 - y, x), "dp": d}
-    up_dev = {"cls": jnp.minimum(cls + 4, n_cls - 1) * 0 + (cls + 4) % n_cls, "dp": d}
+    up_dev = {"cls": (cls + 4) % n_cls, "dp": d}
     down_dev = {"cls": (cls + n_cls - 4) % n_cls, "dp": d}
     core_dev = {"cls": cls, "dp": other}
+
+    def greet(dev):
+        pl.semaphore_signal(barrier, inc=1, device_id=dev, device_id_type=MESH)
+
+    for dev in (x_dev, y_dev, core_dev):
+        greet(dev)
+    pl.when(z < PLANES - 1)(lambda: greet(up_dev))
+    pl.when(z > 0)(lambda: greet(down_dev))
+    lines = 5 - jnp.where(z == 0, 1, 0) - jnp.where(z == PLANES - 1, 1, 0)
+    pl.semaphore_wait(barrier, lines)
 
     def slot(b):
         return d * n_cls + b
@@ -414,7 +417,7 @@
     width = pixels + LANES
     dma = pltpu.SemaphoreType.DMA
     vmem = pl.BlockSpec(memory_space=pltpu.VMEM)
-    return pl.pallas_call(
+    sums, totals = pl.pallas_call(
         functools.partial(dense_kernel, rows_dev, pixels, half, pad, side, n_cls),
         out_shape=(
             jax.ShapeDtypeStruct((1, half, pixels), jnp.float32),
@@ -447,6 +450,7 @@
             collective_id=0, has_side_effects=True, vmem_limit_bytes=56 << 20
         ),
     )(own, references)
+    return sums, totals
 
 
 def solution(mesh):

time: 59.1 us -> 57.4 us (0.971)
  Pallas kernels: 52.2 us -> 50.4 us
    pallas_call x1, Pallas kernels: 52.2 us -> 50.4 us  [dense_on_device(): pl.pallas_call(functools.partial(dense_kernel, rows_dev, pixels, half, pa...]
where the time goes in v1:
time: 57.4 us; the launch traced here: 57.2 us
  Pallas kernels  50.4 us (88%)
  local copies, waits for them, and re-layouts  4.33 us (8%)
  other arithmetic  1.74 us (3%)
  between operations  0.65 us (1%)
    pallas_call x1, Pallas kernels, dense_on_device(): pl.pallas_call(functools.partial(dense_kernel, rows_dev, pixels, half, pa...  50.4 us
    pallas_call x1, local copies, waits for them, and re-layouts, dense_on_device(): pl.pallas_call(functools.partial(dense_kernel, rows_dev, pixels, half, pa...  2.51 us
    unnamed x6, local copies, waits for them, and re-layouts  1.83 us
    concatenate x1, other arithmetic, dense_on_device(): own = jnp.concatenate([images, meta], axis=1)  1.57 us

profile of v1, /device:TPU:0, one launch (start us, length us, event | category | flops | bytes accessed | tf_op | source)
XLA Modules:
  0.0 57.2 jit_solution(11633637613178570193)
XLA Ops:
  0.6 0.8 %copy.8 = s32[16,8]{1,0:T(8,128)S(1)} copy(s32[16,8]{0,1:T(8,128)} %param.6) | data formatting | bytes 1024 | tf_op args[2]
  1.4 0.0 copy-start
  1.4 0.1 fusion
  1.5 0.6 copy-done
  2.0 0.1 broadcast_select_fusion
  2.1 1.6 %pad_maximum_fusion.own_ref = bf16[16,4224]{1,0:T(8,128)(2,1)} fusion(bf16[16,128]{1,0:T(8,128)(2,1)S(1)} %broadcast_select_fusion, bf16[16,4096]{1,0:T(8,128)(2,1)} %param.4), kind=kLoop, calls=%fused_computation | loop fusion | flops 270336 | bytes 270336 | tf_op jit(solution)/shard_map/concatenate | solution.py:416
  3.7 50.4 %shard_map.59 = (f32[1,36,4096]{2,1,0:T(8,128)}, f32[1,36]{1,0:T(1,128)}) custom-call(bf16[16,4224]{1,0:T(8,128)(2,1)} %pad_maximum_fusion.own_ref, bf16[1,72,4096]{2,1,0:T(8,128)(2,1)} %ref_ref.1), custom_call_target="tpu_custom_call" | custom-call | tf_op jit(solution)/shard_map/pallas_call | solution.py:420
  54.1 0.0 copy-start.1
  54.1 2.5 %copy.9 = f32[1,36,4096]{2,0,1:T(1,128)} copy(f32[1,36,4096]{2,1,0:T(8,128)} %get-tuple-element.4) | data formatting | bytes 1179648 | tf_op jit(solution)/shard_map/pallas_call | solution.py:420
  56.6 0.0 copy-done.1
  56.6 0.5 copy.11
Async XLA Ops:
  1.4 0.7 %copy-start = (bf16[16]{0:T(256)(128)(2,1)S(1)}, bf16[16]{0:T(256)(128)(2,1)}, u32[]{:S(2)}) copy-start(bf16[16]{0:T(256)(128)(2,1)} %param.7) | copy-start | bytes 100
  54.1 2.5 %copy-start.1 = (f32[1,36]{1,0:T(1,128)S(1)}, f32[1,36]{1,0:T(1,128)}, u32[]{:S(2)}) copy-start(f32[1,36]{1,0:T(1,128)} %get-tuple-element.9) | copy-start | bytes 436

commit v2 on v1

--- a/solution.py
+++ b/solution.py
@@ -187,9 +187,17 @@
             src_ref=src, dst_ref=dst, send_sem=send, recv_sem=recv, device_id=dev, device_id_type=MESH
         )
 
-    def full(k, which, b, dev):
+    pieces = (part_a, part_b)
+
+    def full(k, h, which, b, dev):
         src = own_ref if k == 0 else held.at[slot(b)]
-        return remote(src, held.at[slot(b)], col_send.at[k, which], col_recv.at[b], dev)
+        return remote(
+            src.at[:, pieces[h]], held.at[slot(b), :, pieces[h]], col_send.at[k, h, which], col_recv.at[h, b], dev
+        )
+
+    def arrived(h, b, dev):
+        ref = held.at[slot(b), :, pieces[h]]
+        remote(ref, ref, col_send.at[0, h, 0], col_recv.at[h, b], dev).wait_recv()
 
     def to_core(index, b, src=None):
         src = held.at[slot(b)] if src is None else src
@@ -208,7 +216,7 @@
         else:
             pl.when(cond)(lambda: copy.start())
 
-    def column_sends(k):
+    def column_sends(k, h):
         b = block(order[k], y, x)
         zk = order[k]
         if k == 0:
@@ -216,11 +224,12 @@
         else:
             up = jnp.logical_and(zk < z, z < PLANES - 1)
             down = jnp.logical_and(zk > z, z > 0)
-        go(full(k, 2, b, up_dev), up)
-        go(full(k, 3, b, down_dev), down)
-        go(full(k, 0, b, x_dev))
-        go(full(k, 1, b, y_dev))
-        go(to_core(k, b, own_ref if k == 0 else None))
+        go(full(k, h, 2, b, up_dev), up)
+        go(full(k, h, 3, b, down_dev), down)
+        go(full(k, h, 0, b, x_dev))
+        go(full(k, h, 1, b, y_dev))
+        if h == 1:
+            go(to_core(k, b, own_ref if k == 0 else None))
 
     count = len(OFFSETS)
 
@@ -268,22 +277,26 @@
 
     local = pltpu.make_async_copy(own_ref, held.at[slot(cls)], own_sem)
     local.start()
-    column_sends(0)
+    column_sends(0, 0)
+    column_sends(0, 1)
     pick_rows()
     build([0])
     for k in range(PLANES):
         xb = block(order[k], y, 1 - x)
-        full(k, 0, xb, x_dev).wait_recv() if k else remote(held.at[slot(xb)], held.at[slot(xb)], col_send.at[0, 0], col_recv.at[xb], x_dev).wait_recv()
-        go(piece(xb, part_b, x_send.at[k], b_recv, y_dev))
-        go(to_core(PLANES + k, xb))
         yb = block(order[k], 1 - y, x)
-        remote(held.at[slot(yb)], held.at[slot(yb)], col_send.at[0, 1], col_recv.at[yb], y_dev).wait_recv()
-        go(piece(yb, part_a, y_send.at[k], a_recv, x_dev))
-        go(to_core(2 * PLANES + k, yb))
-        if k + 1 < PLANES:
-            zb = block(order[k + 1], y, x)
-            remote(held.at[slot(zb)], held.at[slot(zb)], col_send.at[0, 2], col_recv.at[zb], up_dev).wait_recv()
-            column_sends(k + 1)
+        for h in range(2):
+            if k + 1 < PLANES:
+                arrived(h, block(order[k + 1], y, x), up_dev)
+                column_sends(k + 1, h)
+            arrived(h, xb, x_dev)
+            if h == 1:
+                go(piece(xb, part_b, x_send.at[k], b_recv, y_dev))
+                go(to_core(PLANES + k, xb))
+            arrived(h, yb, y_dev)
+            if h == 0:
+                go(piece(yb, part_a, y_send.at[k], a_recv, x_dev))
+            else:
+                go(to_core(2 * PLANES + k, yb))
         build([k + 1])
     for k in range(PLANES):
         b = block(order[k], 1 - y, 1 - x)
@@ -435,8 +448,8 @@
             pltpu.VMEM((2, n_all), jnp.float32),
             pltpu.VMEM((n_cls * n_dp, 2, n_all), jnp.float32),
             dma,
-            dma((PLANES, 4)),
-            dma((n_cls,)),
+            dma((PLANES, 2, 4)),
+            dma((2, n_cls)),
             dma((PLANES,)),
             dma((PLANES,)),
             dma((n_cls,)),

time: 57.4 us -> 52.8 us (0.920)
  Pallas kernels: 50.4 us -> 45.8 us
    pallas_call x1, Pallas kernels: 50.4 us -> 45.8 us  [dense_on_device(): pl.pallas_call(functools.partial(dense_kernel, rows_dev, pixels, half, pa...]
where the time goes in v2:
time: 52.8 us; the launch traced here: 52.5 us
  Pallas kernels  45.8 us (87%)
  local copies, waits for them, and re-layouts  4.33 us (8%)
  other arithmetic  1.74 us (3%)
  between operations  0.65 us (1%)
    pallas_call x1, Pallas kernels, dense_on_device(): pl.pallas_call(functools.partial(dense_kernel, rows_dev, pixels, half, pa...  45.8 us
    pallas_call x1, local copies, waits for them, and re-layouts, dense_on_device(): pl.pallas_call(functools.partial(dense_kernel, rows_dev, pixels, half, pa...  2.51 us
    unnamed x6, local copies, waits for them, and re-layouts  1.83 us
    concatenate x1, other arithmetic, dense_on_device(): own = jnp.concatenate([images, meta], axis=1)  1.57 us

profile of v2, /device:TPU:0, one launch (start us, length us, event | category | flops | bytes accessed | tf_op | source)
XLA Modules:
  0.0 52.5 jit_solution(14351960596541295714)
XLA Ops:
  0.6 0.8 %copy.8 = s32[16,8]{1,0:T(8,128)S(1)} copy(s32[16,8]{0,1:T(8,128)} %param.6) | data formatting | bytes 1024 | tf_op args[2]
  1.4 0.0 copy-start
  1.4 0.1 fusion
  1.5 0.6 %copy-done = bf16[16]{0:T(256)(128)(2,1)S(1)} copy-done((bf16[16]{0:T(256)(128)(2,1)S(1)}, bf16[16]{0:T(256)(128)(2,1)}, u32[]{:S(2)}) %copy-start) | copy-done | bytes 56
  2.0 0.1 broadcast_select_fusion
  2.1 1.6 %pad_maximum_fusion.own_ref = bf16[16,4224]{1,0:T(8,128)(2,1)} fusion(bf16[16,128]{1,0:T(8,128)(2,1)S(1)} %broadcast_select_fusion, bf16[16,4096]{1,0:T(8,128)(2,1)} %param.4), kind=kLoop, calls=%fused_computation | loop fusion | flops 270336 | bytes 270336 | tf_op jit(solution)/shard_map/concatenate | solution.py:429
  3.7 45.8 %shard_map.59 = (f32[1,36,4096]{2,1,0:T(8,128)}, f32[1,36]{1,0:T(1,128)}) custom-call(bf16[16,4224]{1,0:T(8,128)(2,1)} %pad_maximum_fusion.own_ref, bf16[1,72,4096]{2,1,0:T(8,128)(2,1)} %ref_ref.1), custom_call_target="tpu_custom_call" | custom-call | tf_op jit(solution)/shard_map/pallas_call | solution.py:433
  49.5 0.0 copy-start.1
  49.5 2.5 %copy.9 = f32[1,36,4096]{2,0,1:T(1,128)} copy(f32[1,36,4096]{2,1,0:T(8,128)} %get-tuple-element.4) | data formatting | bytes 1179648 | tf_op jit(solution)/shard_map/pallas_call | solution.py:433
  52.0 0.0 copy-done.1
  52.0 0.5 copy.11
Async XLA Ops:
  1.4 0.7 %copy-start = (bf16[16]{0:T(256)(128)(2,1)S(1)}, bf16[16]{0:T(256)(128)(2,1)}, u32[]{:S(2)}) copy-start(bf16[16]{0:T(256)(128)(2,1)} %param.7) | copy-start | bytes 100
  49.5 2.5 %copy-start.1 = (f32[1,36]{1,0:T(1,128)S(1)}, f32[1,36]{1,0:T(1,128)}, u32[]{:S(2)}) copy-start(f32[1,36]{1,0:T(1,128)} %get-tuple-element.9) | copy-start | bytes 436

commit v3 on v2

--- a/solution.py
+++ b/solution.py
@@ -322,7 +322,7 @@
     meta = held[:, :, pixels:pixels + LANES].reshape(n_all, LANES)
     pick = (lax.broadcasted_iota(jnp.int32, (8, LANES), 1) == cls).astype(jnp.float32).astype(jnp.bfloat16)
     noise = lax.dot_general(pick, meta, (((1,), (1,)), ((), ())), preferred_element_type=jnp.float32)[0:1, :]
-    depth = pixels // 8
+    depth = pixels // 4
 
     acc[...] = jnp.zeros_like(acc)
 
@@ -334,7 +334,7 @@
         )
         return carry
 
-    lax.fori_loop(0, 8, chunk, 0)
+    lax.fori_loop(0, 4, chunk, 0)
     rows = count * pad
     prod = acc[0:rows, :].reshape(count, pad, n_all)
     offset = 0.5 * norms[:, 0:1]
@@ -389,7 +389,7 @@
         back[:, cols] = jnp.dot(shifted[:, 0:n_all], right, preferred_element_type=jnp.float32)
         return carry
 
-    lax.fori_loop(0, 8, project, 0)
+    lax.fori_loop(0, 4, project, 0)
 
     place = {offset: i for i, offset in enumerate(OFFSETS)}
 

time: 52.8 us -> 51.3 us (0.972)
  Pallas kernels: 45.8 us -> 44.3 us
    pallas_call x1, Pallas kernels: 45.8 us -> 44.3 us  [dense_on_device(): pl.pallas_call(functools.partial(dense_kernel, rows_dev, pixels, half, pa...]
where the time goes in v3:
time: 51.3 us; the launch traced here: 51.1 us
  Pallas kernels  44.3 us (86%)
  local copies, waits for them, and re-layouts  4.33 us (8%)
  other arithmetic  1.74 us (3%)
  between operations  0.65 us (1%)
    pallas_call x1, Pallas kernels, dense_on_device(): pl.pallas_call(functools.partial(dense_kernel, rows_dev, pixels, half, pa...  44.3 us
    pallas_call x1, local copies, waits for them, and re-layouts, dense_on_device(): pl.pallas_call(functools.partial(dense_kernel, rows_dev, pixels, half, pa...  2.51 us
    unnamed x6, local copies, waits for them, and re-layouts  1.83 us
    concatenate x1, other arithmetic, dense_on_device(): own = jnp.concatenate([images, meta], axis=1)  1.57 us

profile of v3, /device:TPU:0, one launch (start us, length us, event | category | flops | bytes accessed | tf_op | source)
XLA Modules:
  0.0 51.1 jit_solution(13591100259404798945)
XLA Ops:
  0.6 0.8 %copy.8 = s32[16,8]{1,0:T(8,128)S(1)} copy(s32[16,8]{0,1:T(8,128)} %param.6) | data formatting | bytes 1024 | tf_op args[2]
  1.4 0.0 copy-start
  1.4 0.1 fusion
  1.5 0.6 %copy-done = bf16[16]{0:T(256)(128)(2,1)S(1)} copy-done((bf16[16]{0:T(256)(128)(2,1)S(1)}, bf16[16]{0:T(256)(128)(2,1)}, u32[]{:S(2)}) %copy-start) | copy-done | bytes 56
  2.0 0.1 broadcast_select_fusion
  2.1 1.6 %pad_maximum_fusion.own_ref = bf16[16,4224]{1,0:T(8,128)(2,1)} fusion(bf16[16,128]{1,0:T(8,128)(2,1)S(1)} %broadcast_select_fusion, bf16[16,4096]{1,0:T(8,128)(2,1)} %param.4), kind=kLoop, calls=%fused_computation | loop fusion | flops 270336 | bytes 270336 | tf_op jit(solution)/shard_map/concatenate | solution.py:429
  3.7 44.3 %shard_map.59 = (f32[1,36,4096]{2,1,0:T(8,128)}, f32[1,36]{1,0:T(1,128)}) custom-call(bf16[16,4224]{1,0:T(8,128)(2,1)} %pad_maximum_fusion.own_ref, bf16[1,72,4096]{2,1,0:T(8,128)(2,1)} %ref_ref.1), custom_call_target="tpu_custom_call" | custom-call | tf_op jit(solution)/shard_map/pallas_call | solution.py:433
  48.0 0.0 copy-start.1
  48.0 2.5 %copy.9 = f32[1,36,4096]{2,0,1:T(1,128)} copy(f32[1,36,4096]{2,1,0:T(8,128)} %get-tuple-element.4) | data formatting | bytes 1179648 | tf_op jit(solution)/shard_map/pallas_call | solution.py:433
  50.5 0.0 copy-done.1
  50.5 0.5 copy.11
Async XLA Ops:
  1.4 0.7 %copy-start = (bf16[16]{0:T(256)(128)(2,1)S(1)}, bf16[16]{0:T(256)(128)(2,1)}, u32[]{:S(2)}) copy-start(bf16[16]{0:T(256)(128)(2,1)} %param.7) | copy-start | bytes 100
  48.0 2.5 %copy-start.1 = (f32[1,36]{1,0:T(1,128)S(1)}, f32[1,36]{1,0:T(1,128)}, u32[]{:S(2)}) copy-start(f32[1,36]{1,0:T(1,128)} %get-tuple-element.9) | copy-start | bytes 436
